TPU v7x, 32 devices: a whole 2x2x4 slice. The times are simulated.
32 devices in a mesh: comp: 2 (over y), gx: 8 (over z, core), gy: 2 (over x).
Axes of the slice: x: 2, y: 2, z: 4, core: 2. Of those that a mesh axis runs over, the one named last changes fastest.
Arguments:
- state: float32 [2, 7, 256, 64, 128], P('comp', None, 'gx', 'gy'), may hold values from -6 to 6
- diffusivity: float32 [2, 7], replicated, may hold values from 0.01 to 0.06
- advection: float32 [2, 7], replicated, may hold values from 0.05 to 0.3
- solid_mask: int32 [256, 64, 128], P('gx', 'gy'), may hold values 0 or 1
- iface_map: int32 [64], P('gy'), may hold values from 0 to 63, each once
Outputs:
- new_state: float32 [2, 7, 256, 64, 128], P('comp', None, 'gx', 'gy')
Inputs may be any that keep to these rules, and one draw needn't show every extreme that they name: `iface_map`: each turbine inlet row takes exactly one combustor exit-plane row, and every exit-plane row is taken once.
All inputs are finite; a program needn't handle non-finite values. No bound on the sum of `solid_mask` on one device may be relied on, other than what follows from the above.
Results may differ from a plain program's by a relative error of at most 0.0014.
Values may be sent and summed in bfloat16 or wider, within the bound.
No kernel may reach another device: no remote copies, remote signals or barrier semaphores. Data moves between devices by JAX's collectives and lax.ppermute only.
A program may use at most 64 MiB of HBM per device.

v0:
```python
import jax
import jax.numpy as jnp
from jax import lax
from jax.sharding import PartitionSpec as P

RATIO = 1.5
GAIN = 0.4


def swapped(block, axis, apart):
    count = lax.axis_size(axis)
    route = []
    for low in range(count):
        high = low | 1 << apart
        if high != low and high < count:
            route += [(low, high), (high, low)]
    return lax.ppermute(block, axis, route)


def extended(block, sides, width):
    for axis, dim in sides:
        count = lax.axis_size(axis)
        forward = [(i, i + 1) for i in range(count - 1)]
        forward.append((count - 1, 0))
        backward = [(target, source) for source, target in forward]
        low = lax.ppermute(
            lax.slice_in_dim(block, block.shape[dim] - width, None, axis=dim), axis, forward
        )
        high = lax.ppermute(lax.slice_in_dim(block, 0, width, axis=dim), axis, backward)
        block = jnp.concatenate([low, block, high], axis=dim)
    return block


def rates(padded, solid, diff, speed):
    gfac = jnp.exp(GAIN * jnp.tanh(padded[4]))[None]
    mid = padded[:, 1:-1, 1:-1]
    east = padded[:, 2:, 1:-1]
    west = padded[:, :-2, 1:-1]
    north = padded[:, 1:-1, 2:]
    south = padded[:, 1:-1, :-2]
    gmid = gfac[:, 1:-1, 1:-1]
    geast = gfac[:, 2:, 1:-1]
    gwest = gfac[:, :-2, 1:-1]
    gnorth = gfac[:, 1:-1, 2:]
    gsouth = gfac[:, 1:-1, :-2]
    upper = jnp.roll(mid, -1, 3)
    lower = jnp.roll(mid, 1, 3)
    gupper = jnp.roll(gmid, -1, 3)
    glower = jnp.roll(gmid, 1, 3)
    along_x = 0.5 * (gmid + geast) * (east - mid) - 0.5 * (gmid + gwest) * (mid - west)
    along_y = 0.5 * (gmid + gnorth) * (north - mid) - 0.5 * (gmid + gsouth) * (mid - south)
    along_z = 0.5 * (gmid + gupper) * (upper - mid) - 0.5 * (gmid + glower) * (mid - lower)
    diffusion = along_x + along_y + along_z
    dcol = diff[:, None, None, None]
    scol = speed[:, None, None, None]
    fluid = dcol * diffusion - scol * (0.5 * (east - west))
    return jnp.where(solid[None], RATIO * dcol * diffusion, fluid)


def set_edges(padded, first_row, last_row, left_value, on_left, on_right):
    padded = padded.at[:, first_row].set(jnp.where(on_left, left_value, padded[:, first_row]))
    return padded.at[:, last_row].set(
        jnp.where(on_right, jnp.zeros_like(left_value), padded[:, last_row])
    )


def edge_rows(interface, map_whole, row_ids, turbine):
    inflow = jnp.take(interface, jnp.take(map_whole, row_ids), axis=1)
    matches = map_whole[None, :] == row_ids[:, None]
    counting = jnp.arange(map_whole.shape[0], dtype=jnp.int32)[None, :]
    anchor = jnp.sum(jnp.where(matches, counting, 0), axis=1)
    backflow = jnp.take(interface, anchor, axis=1)
    return jnp.where(turbine, inflow, backflow)


def body(state, diffusivity, advection, solid_mask, iface_map):
    fields = state[0]
    comp_pos = lax.axis_index("comp")
    turbine = comp_pos == 1
    diff = lax.dynamic_index_in_dim(diffusivity, comp_pos, 0, keepdims=False)
    speed_raw = lax.dynamic_index_in_dim(advection, comp_pos, 0, keepdims=False)
    speed = jnp.where(turbine, speed_raw, -speed_raw)
    stream_pos = lax.axis_index("gx")
    last_block = lax.axis_size("gx") - 1
    on_left = stream_pos == 0
    on_right = stream_pos == last_block
    solid = (solid_mask == 1) & turbine
    across = swapped(fields[:, 0].astype(jnp.bfloat16), "comp", 0).astype(jnp.float32)
    interface = lax.all_gather(across.astype(jnp.bfloat16), "gy", axis=1, tiled=True).astype(
        across.dtype
    )
    map_whole = lax.all_gather(iface_map, "gy", axis=0, tiled=True)
    rows_dev = fields.shape[2]
    row_base = lax.axis_index("gy") * rows_dev
    row_ids = row_base + jnp.arange(rows_dev, dtype=jnp.int32)
    left_value = edge_rows(interface, map_whole, row_ids, turbine)
    left_full = jnp.pad(left_value, ((0, 0), (1, 1), (0, 0)))

    def with_rim(block):
        padded = extended(block.astype(jnp.bfloat16), (("gx", 1), ("gy", 2)), 1).astype(block.dtype)
        return set_edges(padded, 0, -1, left_full, on_left, on_right)

    first = fields + rates(with_rim(fields), solid, diff, speed)
    second = rates(with_rim(first), solid, diff, speed)
    result = 0.5 * fields + 0.5 * (first + second)
    return result[None]


def solution(mesh):
    return jax.shard_map(
        body,
        mesh=mesh,
        in_specs=(P("comp", None, "gx", "gy", None), P(), P(), P("gx", "gy", None), P("gy")),
        out_specs=P("comp", None, "gx", "gy", None),
        check_vma=False,
    )
```

profile of v0, /device:TPU:0, one launch (start us, length us, event | category | flops | bytes accessed | tf_op | source)
XLA Modules:
  0.0 103.4 jit_solution(14877481706035770598)
XLA Ops:
  0.0 5.4 %copy.31 = bf16[1,7,32,32,128]{4,1,3,2,0:T(8,128)(2,1)S(1)} copy(f32[1,7,32,32,128]{4,3,2,1,0:T(8,128)} %param.15) | data formatting | bytes 5505024 | tf_op args[0]
  5.4 3.0 %collective-permute-start.4 = (bf16[7,32,128]{2,0,1:T(8,128)(2,1)S(1)}, bf16[7,32,128]{2,0,1:T(8,128)(2,1)S(1)}, u32[]{:S(2)}, u32[]{:S(2)}) collective-permute-start(bf16[7,32,128]{2,0,1:T(8,128)(2,1)S(1)} %get-tuple-element.74), channel_id=1, source_target_pairs={{0,16},{16,0},{1,17},{17,1},{2,18},{18,2},{3,19},{19,3},{4,20},{20... | collective-permute-start | bytes 172040 | tf_op jit(solution)/shard_map/ppermute | solution.py:17
  8.5 2.8 %collective-permute-start.1 = (bf16[7,1,32,128]{3,0,2,1:T(8,128)(2,1)S(1)}, bf16[7,1,32,128]{3,0,2,1:T(8,128)(2,1)S(1)}, u32[]{:S(2)}, u32[]{:S(2)}) collective-permute-start(bf16[7,1,32,128]{3,0,2,1:T(8,128)(2,1)S(1)} %get-tuple-element.75), channel_id=1, source_target_pairs={{2,0},{4,2},{6,4},{8,6},{10,8},{12,10},{14,12},{0,14},{3,1},{5,3},... | collective-permute-start | bytes 172040 | tf_op jit(solution)/shard_map/ppermute | solution.py:29
  12.8 4.3 %all-reduce.1 = s32[64]{0:T(128)S(1)} all-reduce(s32[64]{0:T(128)S(1)} %dynamic-update-slice.12), channel_id=1, replica_groups=mesh['comp'=2,'gx'=8,'gy'=2] {'gy'}, use_global_device_ids=true, to_apply=%add.1 | all-reduce | flops 64 | bytes 512
  18.2 5.6 %all_gather.6 = bf16[7,64,128]{2,1,0:T(8,128)(2,1)S(1)} all-gather(bf16[7,32,128]{2,1,0:T(8,128)(2,1)S(1)} %copy.19), channel_id=1, replica_groups=mesh['comp'=2,'gx'=8,'gy'=2] {'gy'}, dimensions={1}, use_global_device_ids=true | all-gather | bytes 172032 | tf_op jit(solution)/shard_map/all_gather | solution.py:89
  23.9 1.6 %collective-permute-start.2 = (bf16[7,34,1,128]{3,0,2,1:T(8,128)(2,1)S(1)}, bf16[7,34,1,128]{3,0,2,1:T(8,128)(2,1)S(1)}, u32[]{:S(2)}, u32[]{:S(2)}) collective-permute-start(bf16[7,34,1,128]{3,0,2,1:T(8,128)(2,1)S(1)} %get-tuple-element.70), channel_id=1, source_target_pairs={{0,1},{1,0},{2,3},{3,2},{4,5},{5,4},{6,7},{7,6},{8,9},{9,8},{10,11... | collective-permute-start | bytes 182792 | tf_op jit(solution)/shard_map/ppermute | solution.py:26
  28.3 1.5 %collective-permute-done.3 = bf16[7,34,1,128]{3,0,2,1:T(8,128)(2,1)S(1)} collective-permute-done((bf16[7,34,1,128]{3,0,2,1:T(8,128)(2,1)S(1)}, bf16[7,34,1,128]{3,0,2,1:T(8,128)(2,1)S(1)}, u32[]{:S(2)}, u32[]{:S(2)}) %collective-permute-start.3) | collective-permute-done | bytes 60960 | tf_op jit(solution)/shard_map/ppermute | solution.py:29
  29.8 1.3 %maximum_convert_fusion = f32[7,34,34,128]{3,0,2,1:T(8,128)S(1)} fusion(bf16[7,34,1,128]{3,0,2,1:T(8,128)(2,1)S(1)} %collective-permute-done.3, bf16[7,1,32,128]{3,0,2,1:T(8,128)(2,1)S(1)} %collective-permute-done.1, bf16[7,32,32,128]{3,0,2,1:T(8,128)(2,1)S(1)} %bitcast.66, bf16[7,1,32,128]{3,0,2,1:T(8,128)(2,1)S(1)} %collective-permute-done, ...), kind=kLoop, calls=%fused_computation.32 | loop fusion | flops 5178880 | bytes 6214656 | tf_op jit(solution)/shard_map/convert_element_type | solution.py:100
  31.2 1.2 %fusion.21 = f32[1,34,34,128]{3,0,2,1:T(1,128)S(1)} fusion(f32[7,34,34,128]{3,0,2,1:T(8,128)S(1)} %fusion.38), kind=kLoop, calls=%fused_computation.39 | loop fusion | flops 147968 | bytes 1183744 | tf_op jit(solution)/shard_map/exp | solution.py:35
  34.7 3.5 %fusion.51 = (f32[7,32,32,1]{3,0,2,1:T(8,128)S(1)}, f32[7,32,32,1]{3,0,2,1:T(8,128)}) fusion(f32[7,34,34,128]{3,0,2,1:T(8,128)S(1)} %fusion.38), kind=kLoop, calls=%fused_computation.110 | loop fusion | bytes 114688 | tf_op jit(solution)/shard_map/jit(_roll_static)/slice | solution.py:46
  38.2 4.8 %fusion.50 = (f32[7,32,32,127]{3,0,2,1:T(8,128)}, f32[7,32,32,127]{3,0,2,1:T(8,128)}) fusion(f32[7,34,34,128]{3,0,2,1:T(8,128)S(1)} %fusion.38), kind=kLoop, calls=%fused_computation.109 | loop fusion | bytes 14565376 | tf_op jit(solution)/shard_map/jit(_roll_static)/slice | solution.py:46
  43.1 4.4 %fusion.29 = (f32[1,32,32,128]{3,0,2,1:T(1,128)S(1)}, f32[1,32,32,128]{3,0,2,1:T(1,128)S(1)}, f32[1,32,32,128]{3,0,2,1:T(1,128)S(1)}, f32[1,32,32,128]{3,0,2,1:T...) fusion(f32[1,34,34,128]{3,0,2,1:T(1,128)S(1)} %fusion.21, ...), kind=kLoop, calls=%fused_computation.55 | loop fusion | flops 1835008 | bytes 6815744 | tf_op jit(solution)/shard_map/mul | solution.py:50
  47.5 11.8 %fusion.46 = (bf16[7,32,32,128]{3,0,2,1:T(8,128)(2,1)S(1)}, f32[7,32,32,128]{3,0,2,1:T(8,128)S(1)}) fusion(f32[7]{0:T(128)S(1)} %fusion.42, f32[7]{0:T(128)S(1)} %get-tuple-element.57, f32[7,32,32,127]{3,0,2,1:T(8,128)} %get-tuple-element.65, f32[7,32,32,1]{3,0,2,1:T(8,128)} %get-tuple-element.67, f32[32,32,128]{2,1,0:T(8,128)S(1)} %bitcast.74, ...), kind=kLoop, calls=%fused_computation.106 | loop fusion | flops 24772608 | bytes 38142036 | tf_op jit(solution)/shard_map/convert_element_type | solution.py:100
  59.4 3.5 %collective-permute-start.6 = (bf16[7,1,32,128]{3,0,2,1:T(8,128)(2,1)S(1)}, bf16[7,1,32,128]{3,0,2,1:T(8,128)(2,1)S(1)}, u32[]{:S(2)}, u32[]{:S(2)}) collective-permute-start(bf16[7,1,32,128]{3,0,2,1:T(8,128)(2,1)S(1)} %get-tuple-element.73), channel_id=1, source_target_pairs={{2,0},{4,2},{6,4},{8,6},{10,8},{12,10},{14,12},{0,14},{3,1},{5,3},... | collective-permute-start | bytes 172040 | tf_op jit(solution)/shard_map/ppermute | solution.py:29
  62.9 2.1 %collective-permute-done.5 = bf16[7,1,32,128]{3,0,2,1:T(8,128)(2,1)S(1)} collective-permute-done((bf16[7,1,32,128]{3,0,2,1:T(8,128)(2,1)S(1)}, bf16[7,1,32,128]{3,0,2,1:T(8,128)(2,1)S(1)}, u32[]{:S(2)}, u32[]{:S(2)}) %collective-permute-start.5) | collective-permute-done | bytes 57376 | tf_op jit(solution)/shard_map/ppermute | solution.py:26
  65.1 1.2 %collective-permute-start.7 = (bf16[7,34,1,128]{3,0,2,1:T(8,128)(2,1)S(1)}, bf16[7,34,1,128]{3,0,2,1:T(8,128)(2,1)S(1)}, u32[]{:S(2)}, u32[]{:S(2)}) collective-permute-start(bf16[7,34,1,128]{3,0,2,1:T(8,128)(2,1)S(1)} %get-tuple-element.68), channel_id=1, source_target_pairs={{0,1},{1,0},{2,3},{3,2},{4,5},{5,4},{6,7},{7,6},{8,9},{9,8},{10,11... | collective-permute-start | bytes 182792 | tf_op jit(solution)/shard_map/ppermute | solution.py:26
  67.1 2.3 %collective-permute-done.7 = bf16[7,34,1,128]{3,0,2,1:T(8,128)(2,1)S(1)} collective-permute-done((bf16[7,34,1,128]{3,0,2,1:T(8,128)(2,1)S(1)}, bf16[7,34,1,128]{3,0,2,1:T(8,128)(2,1)S(1)}, u32[]{:S(2)}, u32[]{:S(2)}) %collective-permute-start.7) | collective-permute-done | bytes 60960 | tf_op jit(solution)/shard_map/ppermute | solution.py:26
  70.6 1.3 %maximum_convert_fusion.1 = f32[7,34,34,128]{3,0,2,1:T(8,128)S(1)} fusion(bf16[7,34,1,128]{3,0,2,1:T(8,128)(2,1)S(1)} %collective-permute-done.8, bf16[7,1,32,128]{3,0,2,1:T(8,128)(2,1)S(1)} %collective-permute-done.6, bf16[7,32,32,128]{3,0,2,1:T(8,128)(2,1)S(1)} %get-tuple-element.54, bf16[7,1,32,128]{3,0,2,1:T(8,128)(2,1)S(1)} %collective-permute-done.5, ...), kind=kLoop, calls=%fused_computation.33 | loop fusion | flops 5178880 | bytes 6214656 | tf_op jit(solution)/shard_map/convert_element_type | solution.py:100
  72.0 1.2 %fusion.19 = f32[1,34,34,128]{3,0,2,1:T(1,128)S(1)} fusion(f32[7,34,34,128]{3,0,2,1:T(8,128)S(1)} %fusion.34), kind=kLoop, calls=%fused_computation.36 | loop fusion | flops 147968 | bytes 1183744 | tf_op jit(solution)/shard_map/exp | solution.py:35
  75.5 3.5 %fusion.49 = (f32[7,32,32,1]{3,0,2,1:T(8,128)S(1)}, f32[7,32,32,1]{3,0,2,1:T(8,128)}) fusion(f32[7,34,34,128]{3,0,2,1:T(8,128)S(1)} %fusion.34), kind=kLoop, calls=%fused_computation.108 | loop fusion | bytes 114688 | tf_op jit(solution)/shard_map/jit(_roll_static)/slice | solution.py:46
  79.0 4.8 %fusion.48 = (f32[7,32,32,127]{3,0,2,1:T(8,128)}, f32[7,32,32,127]{3,0,2,1:T(8,128)}) fusion(f32[7,34,34,128]{3,0,2,1:T(8,128)S(1)} %fusion.34), kind=kLoop, calls=%fused_computation.107 | loop fusion | bytes 14565376 | tf_op jit(solution)/shard_map/jit(_roll_static)/slice | solution.py:46
  83.9 5.0 %fusion.25 = (f32[1,32,32,128]{3,0,2,1:T(1,128)S(1)}, f32[1,32,32,128]{3,0,2,1:T(1,128)S(1)}, f32[1,32,32,128]{3,0,2,1:T(1,128)S(1)}, f32[1,32,32,128]{3,0,2,1:T...) fusion(f32[1,34,34,128]{3,0,2,1:T(1,128)S(1)} %fusion.19, f32[1,32,32,127]{3,0,2,1:T(1,128)S(1)} %get-tuple-element.84, ...), kind=kLoop, calls=%fused_computation.47 | loop fusion | flops 1835008 | bytes 6815744 | tf_op jit(solution)/shard_map/mul | solution.py:50
  88.8 12.1 %fusion.17 = f32[1,7,32,32,128]{4,1,3,2,0:T(8,128)S(1)} fusion(f32[1,7,32,32,128]{4,3,2,1,0:T(8,128)S(1)} %copy-done, f32[7,32,32,128]{3,0,2,1:T(8,128)S(1)} %get-tuple-element.55, f32[7,32,32,127]{3,0,2,1:T(8,128)} %get-tuple-element.61, f32[7,32,32,1]{3,0,2,1:T(8,128)} %get-tuple-element.63, f32[7,32,32,1]{3,0,2,1:T(8,128)S(1)} %get-tuple-element.62, ...), kind=kLoop, calls=%fused_computation.31 | loop fusion | flops 25690112 | bytes 39977044 | tf_op jit(solution)/shard_map/broadcast_in_dim | solution.py:106
  100.9 2.5 %copy.21 = f32[1,7,32,32,128]{4,3,2,1,0:T(8,128)} copy(f32[1,7,32,32,128]{4,1,3,2,0:T(8,128)S(1)} %fusion.17) | data formatting | bytes 7340032 | tf_op jit(solution)/shard_map/broadcast_in_dim | solution.py:106
  (57 shorter events, 11.6 us)
Async XLA Ops:
  0.0 11.3 %copy-start.6 = (u32[32]{0:T(128)S(1)}, u32[32]{0:T(128)}, u32[]{:S(2)}) copy-start(u32[32]{0:T(128)} %constant.162) | copy-start | bytes 388
  0.0 12.5 %copy-start.5 = (s32[32]{0:T(128)S(1)}, s32[32]{0:T(128)}, u32[]{:S(2)}) copy-start(s32[32]{0:T(128)} %param.19) | copy-start | bytes 388
  0.0 18.0 %copy-start.3 = (f32[2,7]{1,0:T(2,128)S(1)}, f32[2,7]{1,0:T(2,128)}, u32[]{:S(2)}) copy-start(f32[2,7]{1,0:T(2,128)} %param.16) | copy-start | bytes 172
  0.0 18.0 %copy-start.2 = (s32[32,32,128]{2,1,0:T(8,128)S(1)}, s32[32,32,128]{2,1,0:T(8,128)}, u32[]{:S(2)}) copy-start(s32[32,32,128]{2,1,0:T(8,128)} %param.18) | copy-start | bytes 1572868
  0.0 18.1 %copy-start.4 = (f32[2,7]{1,0:T(2,128)S(1)}, f32[2,7]{1,0:T(2,128)}, u32[]{:S(2)}) copy-start(f32[2,7]{1,0:T(2,128)} %param.17) | copy-start | bytes 172
  5.4 12.7 %collective-permute-start.4 = (bf16[7,32,128]{2,0,1:T(8,128)(2,1)S(1)}, bf16[7,32,128]{2,0,1:T(8,128)(2,1)S(1)}, u32[]{:S(2)}, u32[]{:S(2)}) collective-permute-start(bf16[7,32,128]{2,0,1:T(8,128)(2,1)S(1)} %get-tuple-element.74), channel_id=1, source_target_pairs={{0,16},{16,0},{1,17},{17,1},{2,18},{18,2},{3,19},{19,3},{4,20},{20... | collective-permute-start | bytes 172040 | tf_op jit(solution)/shard_map/ppermute | solution.py:17
  8.5 15.4 %collective-permute-start.1 = (bf16[7,1,32,128]{3,0,2,1:T(8,128)(2,1)S(1)}, bf16[7,1,32,128]{3,0,2,1:T(8,128)(2,1)S(1)}, u32[]{:S(2)}, u32[]{:S(2)}) collective-permute-start(bf16[7,1,32,128]{3,0,2,1:T(8,128)(2,1)S(1)} %get-tuple-element.75), channel_id=1, source_target_pairs={{2,0},{4,2},{6,4},{8,6},{10,8},{12,10},{14,12},{0,14},{3,1},{5,3},... | collective-permute-start | bytes 172040 | tf_op jit(solution)/shard_map/ppermute | solution.py:29
  11.2 12.6 %collective-permute-start = (bf16[7,1,32,128]{3,0,2,1:T(8,128)(2,1)S(1)}, bf16[7,1,32,128]{3,0,2,1:T(8,128)(2,1)S(1)}, u32[]{:S(2)}, u32[]{:S(2)}) collective-permute-start(bf16[7,1,32,128]{3,0,2,1:T(8,128)(2,1)S(1)} %get-tuple-element.76), channel_id=1, source_target_pairs={{0,2},{2,4},{4,6},{6,8},{8,10},{10,12},{12,14},{14,0},{1,3},{3,5},... | collective-permute-start | bytes 172040 | tf_op jit(solution)/shard_map/ppermute | solution.py:26
  18.1 29.4 %copy-start.1 = (pred[32,32,128]{2,1,0:T(8,128)(4,1)}, pred[32,32,128]{2,1,0:T(8,128)(4,1)S(1)}, u32[]{:S(2)}) copy-start(pred[32,32,128]{2,1,0:T(8,128)(4,1)S(1)} %compare_and_fusion) | copy-start | bytes 393220
  23.9 4.4 %collective-permute-start.2 = (bf16[7,34,1,128]{3,0,2,1:T(8,128)(2,1)S(1)}, bf16[7,34,1,128]{3,0,2,1:T(8,128)(2,1)S(1)}, u32[]{:S(2)}, u32[]{:S(2)}) collective-permute-start(bf16[7,34,1,128]{3,0,2,1:T(8,128)(2,1)S(1)} %get-tuple-element.70), channel_id=1, source_target_pairs={{0,1},{1,0},{2,3},{3,2},{4,5},{5,4},{6,7},{7,6},{8,9},{9,8},{10,11... | collective-permute-start | bytes 182792 | tf_op jit(solution)/shard_map/ppermute | solution.py:26
  25.5 4.3 %collective-permute-start.3 = (bf16[7,34,1,128]{3,0,2,1:T(8,128)(2,1)S(1)}, bf16[7,34,1,128]{3,0,2,1:T(8,128)(2,1)S(1)}, u32[]{:S(2)}, u32[]{:S(2)}) collective-permute-start(bf16[7,34,1,128]{3,0,2,1:T(8,128)(2,1)S(1)} %get-tuple-element.71), channel_id=1, source_target_pairs={{1,0},{0,1},{3,2},{2,3},{5,4},{4,5},{7,6},{6,7},{9,8},{8,9},{11,10... | collective-permute-start | bytes 182792 | tf_op jit(solution)/shard_map/ppermute | solution.py:29
  43.1 4.4 %copy-start = (f32[1,7,32,32,128]{4,3,2,1,0:T(8,128)S(1)}, f32[1,7,32,32,128]{4,3,2,1,0:T(8,128)}, u32[]{:S(2)}) copy-start(f32[1,7,32,32,128]{4,3,2,1,0:T(8,128)} %param.15) | copy-start | bytes 11010052
  59.3 5.7 %collective-permute-start.5 = (bf16[7,1,32,128]{3,0,2,1:T(8,128)(2,1)S(1)}, bf16[7,1,32,128]{3,0,2,1:T(8,128)(2,1)S(1)}, u32[]{:S(2)}, u32[]{:S(2)}) collective-permute-start(bf16[7,1,32,128]{3,0,2,1:T(8,128)(2,1)S(1)} %get-tuple-element.72), channel_id=1, source_target_pairs={{0,2},{2,4},{4,6},{6,8},{8,10},{10,12},{12,14},{14,0},{1,3},{3,5},... | collective-permute-start | bytes 172040 | tf_op jit(solution)/shard_map/ppermute | solution.py:26
  59.4 5.6 %collective-permute-start.6 = (bf16[7,1,32,128]{3,0,2,1:T(8,128)(2,1)S(1)}, bf16[7,1,32,128]{3,0,2,1:T(8,128)(2,1)S(1)}, u32[]{:S(2)}, u32[]{:S(2)}) collective-permute-start(bf16[7,1,32,128]{3,0,2,1:T(8,128)(2,1)S(1)} %get-tuple-element.73), channel_id=1, source_target_pairs={{2,0},{4,2},{6,4},{8,6},{10,8},{12,10},{14,12},{0,14},{3,1},{5,3},... | collective-permute-start | bytes 172040 | tf_op jit(solution)/shard_map/ppermute | solution.py:29
  65.1 4.4 %collective-permute-start.7 = (bf16[7,34,1,128]{3,0,2,1:T(8,128)(2,1)S(1)}, bf16[7,34,1,128]{3,0,2,1:T(8,128)(2,1)S(1)}, u32[]{:S(2)}, u32[]{:S(2)}) collective-permute-start(bf16[7,34,1,128]{3,0,2,1:T(8,128)(2,1)S(1)} %get-tuple-element.68), channel_id=1, source_target_pairs={{0,1},{1,0},{2,3},{3,2},{4,5},{5,4},{6,7},{7,6},{8,9},{9,8},{10,11... | collective-permute-start | bytes 182792 | tf_op jit(solution)/shard_map/ppermute | solution.py:26
  66.3 4.3 %collective-permute-start.8 = (bf16[7,34,1,128]{3,0,2,1:T(8,128)(2,1)S(1)}, bf16[7,34,1,128]{3,0,2,1:T(8,128)(2,1)S(1)}, u32[]{:S(2)}, u32[]{:S(2)}) collective-permute-start(bf16[7,34,1,128]{3,0,2,1:T(8,128)(2,1)S(1)} %get-tuple-element.69), channel_id=1, source_target_pairs={{1,0},{0,1},{3,2},{2,3},{5,4},{4,5},{7,6},{6,7},{9,8},{8,9},{11,10... | collective-permute-start | bytes 182792 | tf_op jit(solution)/shard_map/ppermute | solution.py:29
where the time goes:
time: 104 us; the launch traced here: 103 us
  other arithmetic  39.1 us (38%)
  local copies, waits for them, and re-layouts  31.9 us (31%)
  starting transfers between devices  13.6 us (13%)
  blocking collectives  9.9 us (10%)
  waiting for transfers between devices  7.89 us (8%)
    slice x4, local copies, waits for them, and re-layouts, rates(): upper = jnp.roll(mid, -1, 3)  16.7 us
    broadcast_in_dim x1, other arithmetic, body(): return result[None]  12.1 us
    convert_element_type x1, other arithmetic, with_rim(): block.astype(jnp.bfloat16)  11.8 us
    mul x2, other arithmetic, rates(): 0.5 * (gmid + geast) * (east - mid) - 0.5 * (gmid + gwest) * (mid - west)  9.4 us
    ppermute x4, starting transfers between devices, extended(): lax.ppermute(lax.slice_in_dim(block, 0, width, axis=dim), axis, backward)  7.71 us
    unnamed x18, local copies, waits for them, and re-layouts  6.24 us
    all_gather x1, blocking collectives, body(): lax.all_gather(across.astype(jnp.bfloat16), 'gy', axis=1, tiled=True)  5.65 us
    ppermute x4, waiting for transfers between devices, extended(): lax.ppermute(lax.slice_in_dim(block, block.shape[dim] - width, None, axis...  5.25 us
  transfers between devices with their start and end apart: 9, of which 5 were waited for; matrix products, arithmetic and copies ran while one was open for 3% of the time, Pallas kernels for 0%

commit v1 on v0

--- a/solution.py
+++ b/solution.py
@@ -5,6 +5,21 @@
 
 RATIO = 1.5
 GAIN = 0.4
+
+
+def _unite_windows(incoming_x, dev_axis):
+    wide_out = lax.axis_size(dev_axis)
+    top, r1 = (wide_out, lax.axis_index(dev_axis))
+    z, carry_in = (incoming_x, 1)
+    while carry_in < top:
+        item_now = lax.ppermute(
+            z, dev_axis, tuple(((dev_j, dev_j ^ carry_in) for dev_j in range(top)))
+        )
+        base_arr = jnp.concatenate([z, item_now], axis=1)
+        b_next = jnp.concatenate([item_now, z], axis=1)
+        z = jnp.where(r1 & carry_in == 0, base_arr, b_next)
+        carry_in = 2 * carry_in
+    return z
 
 
 def swapped(block, axis, apart):
@@ -86,9 +101,7 @@
     on_right = stream_pos == last_block
     solid = (solid_mask == 1) & turbine
     across = swapped(fields[:, 0].astype(jnp.bfloat16), "comp", 0).astype(jnp.float32)
-    interface = lax.all_gather(across.astype(jnp.bfloat16), "gy", axis=1, tiled=True).astype(
-        across.dtype
-    )
+    interface = _unite_windows(across.astype(jnp.bfloat16), dev_axis="gy").astype(across.dtype)
     map_whole = lax.all_gather(iface_map, "gy", axis=0, tiled=True)
     rows_dev = fields.shape[2]
     row_base = lax.axis_index("gy") * rows_dev

time: 104 us -> 98.9 us (0.951)
  blocking collectives: 9.9 us -> 4.25 us
  starting transfers between devices: 13.6 us -> 15.2 us
    all_gather x1 -> x0, blocking collectives: 5.65 us -> none  [body(): lax.all_gather(across.astype(jnp.bfloat16), 'gy', axis=1, tiled=True)]
    ppermute x0 -> x1, starting transfers between devices: none -> 1.57 us  [_unite_windows(): lax.ppermute(z, dev_axis, tuple(((dev_j, dev_j ^ carry_in) for dev_j in r...]
  transfers between devices with their start and end apart: 9 -> 10, of which waited for: 5 -> 6; matrix products, arithmetic and copies ran while one was open for 3% -> 3% of each run, Pallas kernels for 0% -> 0%
where the time goes in v1:
time: 98.9 us; the launch traced here: 98.7 us
  other arithmetic  39.1 us (40%)
  local copies, waits for them, and re-layouts  32 us (32%)
  starting transfers between devices  15.2 us (15%)
  waiting for transfers between devices  7.27 us (7%)
  blocking collectives  4.25 us (4%)
  between operations  1 us (1%)
    slice x4, local copies, waits for them, and re-layouts, rates(): upper = jnp.roll(mid, -1, 3)  16.7 us
    broadcast_in_dim x1, other arithmetic, body(): return result[None]  12.1 us
    convert_element_type x1, other arithmetic, with_rim(): block.astype(jnp.bfloat16)  11.8 us
    mul x2, other arithmetic, rates(): 0.5 * (gmid + geast) * (east - mid) - 0.5 * (gmid + gwest) * (mid - west)  9.41 us
    ppermute x4, starting transfers between devices, extended(): lax.ppermute(lax.slice_in_dim(block, 0, width, axis=dim), axis, backward)  8.53 us
    unnamed x18, local copies, waits for them, and re-layouts  6.24 us
    ppermute x4, waiting for transfers between devices, extended(): lax.ppermute(lax.slice_in_dim(block, block.shape[dim] - width, None, axis...  4.61 us
    slice x4, local copies, waits for them, and re-layouts, rates(): gupper = jnp.roll(gmid, -1, 3)  4.6 us
  transfers between devices with their start and end apart: 10, of which 6 were waited for; matrix products, arithmetic and copies ran while one was open for 3% of the time, Pallas kernels for 0%

profile of v1, /device:TPU:0, one launch (start us, length us, event | category | flops | bytes accessed | tf_op | source)
XLA Modules:
  0.0 98.7 jit_solution(3038288952328975110)
XLA Ops:
  0.0 5.4 %copy.24 = bf16[1,7,32,32,128]{4,1,3,2,0:T(8,128)(2,1)S(1)} copy(f32[1,7,32,32,128]{4,3,2,1,0:T(8,128)} %param.15) | data formatting | bytes 5505024 | tf_op args[0]
  5.4 3.0 %collective-permute-start.4 = (bf16[7,32,128]{2,0,1:T(8,128)(2,1)S(1)}, bf16[7,32,128]{2,0,1:T(8,128)(2,1)S(1)}, u32[]{:S(2)}, u32[]{:S(2)}) collective-permute-start(bf16[7,32,128]{2,0,1:T(8,128)(2,1)S(1)} %get-tuple-element.74), channel_id=1, source_target_pairs={{0,16},{16,0},{1,17},{17,1},{2,18},{18,2},{3,19},{19,3},{4,20},{20... | collective-permute-start | bytes 172040 | tf_op jit(solution)/shard_map/ppermute | solution.py:32
  8.5 2.8 %collective-permute-start.1 = (bf16[7,1,32,128]{3,0,2,1:T(8,128)(2,1)S(1)}, bf16[7,1,32,128]{3,0,2,1:T(8,128)(2,1)S(1)}, u32[]{:S(2)}, u32[]{:S(2)}) collective-permute-start(bf16[7,1,32,128]{3,0,2,1:T(8,128)(2,1)S(1)} %get-tuple-element.75), channel_id=1, source_target_pairs={{2,0},{4,2},{6,4},{8,6},{10,8},{12,10},{14,12},{0,14},{3,1},{5,3},... | collective-permute-start | bytes 172040 | tf_op jit(solution)/shard_map/ppermute | solution.py:44
  12.8 4.3 %all-reduce.1 = s32[64]{0:T(128)S(1)} all-reduce(s32[64]{0:T(128)S(1)} %dynamic-update-slice.12), channel_id=1, replica_groups=mesh['comp'=2,'gx'=8,'gy'=2] {'gy'}, use_global_device_ids=true, to_apply=%add.1 | all-reduce | flops 64 | bytes 512
  18.2 1.6 %collective-permute-start.5 = (bf16[7,32,128]{2,0,1:T(8,128)(2,1)S(1)}, bf16[7,32,128]{2,0,1:T(8,128)(2,1)S(1)}, u32[]{:S(2)}, u32[]{:S(2)}) collective-permute-start(bf16[7,32,128]{2,0,1:T(8,128)(2,1)S(1)} %collective-permute-done.4), channel_id=1, source_target_pairs={{0,1},{1,0},{2,3},{3,2},{4,5},{5,4},{6,7},{7,6},{8,9},{9,8},{10,11... | collective-permute-start | bytes 172040 | tf_op jit(solution)/shard_map/ppermute | solution.py:15
  20.4 1.5 %collective-permute-start.3 = (bf16[7,34,1,128]{3,0,2,1:T(8,128)(2,1)S(1)}, bf16[7,34,1,128]{3,0,2,1:T(8,128)(2,1)S(1)}, u32[]{:S(2)}, u32[]{:S(2)}) collective-permute-start(bf16[7,34,1,128]{3,0,2,1:T(8,128)(2,1)S(1)} %get-tuple-element.71), channel_id=1, source_target_pairs={{1,0},{0,1},{3,2},{2,3},{5,4},{4,5},{7,6},{6,7},{9,8},{8,9},{11,10... | collective-permute-start | bytes 182792 | tf_op jit(solution)/shard_map/ppermute | solution.py:44
  24.9 1.3 %maximum_convert_fusion = f32[7,34,34,128]{3,0,2,1:T(8,128)S(1)} fusion(bf16[7,34,1,128]{3,0,2,1:T(8,128)(2,1)S(1)} %collective-permute-done.3, bf16[7,1,32,128]{3,0,2,1:T(8,128)(2,1)S(1)} %collective-permute-done.1, bf16[7,32,32,128]{3,0,2,1:T(8,128)(2,1)S(1)} %bitcast.66, bf16[7,1,32,128]{3,0,2,1:T(8,128)(2,1)S(1)} %collective-permute-done, ...), kind=kLoop, calls=%fused_computation.32 | loop fusion | flops 5178880 | bytes 6214656 | tf_op jit(solution)/shard_map/convert_element_type | solution.py:113
  26.3 1.2 %fusion.21 = f32[1,34,34,128]{3,0,2,1:T(1,128)S(1)} fusion(f32[7,34,34,128]{3,0,2,1:T(8,128)S(1)} %fusion.38), kind=kLoop, calls=%fused_computation.39 | loop fusion | flops 147968 | bytes 1183744 | tf_op jit(solution)/shard_map/exp | solution.py:50
  29.9 3.5 %fusion.52 = (f32[7,32,32,1]{3,0,2,1:T(8,128)S(1)}, f32[7,32,32,1]{3,0,2,1:T(8,128)}) fusion(f32[7,34,34,128]{3,0,2,1:T(8,128)S(1)} %fusion.38), kind=kLoop, calls=%fused_computation.111 | loop fusion | bytes 114688 | tf_op jit(solution)/shard_map/jit(_roll_static)/slice | solution.py:61
  33.4 4.8 %fusion.51 = (f32[7,32,32,127]{3,0,2,1:T(8,128)}, f32[7,32,32,127]{3,0,2,1:T(8,128)}) fusion(f32[7,34,34,128]{3,0,2,1:T(8,128)S(1)} %fusion.38), kind=kLoop, calls=%fused_computation.110 | loop fusion | bytes 14565376 | tf_op jit(solution)/shard_map/jit(_roll_static)/slice | solution.py:61
  38.2 4.4 %fusion.29 = (f32[1,32,32,128]{3,0,2,1:T(1,128)S(1)}, f32[1,32,32,128]{3,0,2,1:T(1,128)S(1)}, f32[1,32,32,128]{3,0,2,1:T(1,128)S(1)}, f32[1,32,32,128]{3,0,2,1:T...) fusion(f32[1,34,34,128]{3,0,2,1:T(1,128)S(1)} %fusion.21, ...), kind=kLoop, calls=%fused_computation.55 | loop fusion | flops 1835008 | bytes 6815744 | tf_op jit(solution)/shard_map/mul | solution.py:65
  42.7 11.8 %fusion.47 = (bf16[7,32,32,128]{3,0,2,1:T(8,128)(2,1)S(1)}, f32[7,32,32,128]{3,0,2,1:T(8,128)S(1)}) fusion(f32[7]{0:T(128)S(1)} %fusion.43, f32[7]{0:T(128)S(1)} %get-tuple-element.57, f32[7,32,32,127]{3,0,2,1:T(8,128)} %get-tuple-element.65, f32[7,32,32,1]{3,0,2,1:T(8,128)} %get-tuple-element.67, f32[32,32,128]{2,1,0:T(8,128)S(1)} %bitcast.74, ...), kind=kLoop, calls=%fused_computation.107 | loop fusion | flops 24772608 | bytes 38142036 | tf_op jit(solution)/shard_map/convert_element_type | solution.py:113
  54.6 3.5 %collective-permute-start.7 = (bf16[7,1,32,128]{3,0,2,1:T(8,128)(2,1)S(1)}, bf16[7,1,32,128]{3,0,2,1:T(8,128)(2,1)S(1)}, u32[]{:S(2)}, u32[]{:S(2)}) collective-permute-start(bf16[7,1,32,128]{3,0,2,1:T(8,128)(2,1)S(1)} %get-tuple-element.73), channel_id=1, source_target_pairs={{2,0},{4,2},{6,4},{8,6},{10,8},{12,10},{14,12},{0,14},{3,1},{5,3},... | collective-permute-start | bytes 172040 | tf_op jit(solution)/shard_map/ppermute | solution.py:44
  58.1 2.0 %collective-permute-done.6 = bf16[7,1,32,128]{3,0,2,1:T(8,128)(2,1)S(1)} collective-permute-done((bf16[7,1,32,128]{3,0,2,1:T(8,128)(2,1)S(1)}, bf16[7,1,32,128]{3,0,2,1:T(8,128)(2,1)S(1)}, u32[]{:S(2)}, u32[]{:S(2)}) %collective-permute-start.6) | collective-permute-done | bytes 57376 | tf_op jit(solution)/shard_map/ppermute | solution.py:41
  60.2 1.4 %collective-permute-start.8 = (bf16[7,34,1,128]{3,0,2,1:T(8,128)(2,1)S(1)}, bf16[7,34,1,128]{3,0,2,1:T(8,128)(2,1)S(1)}, u32[]{:S(2)}, u32[]{:S(2)}) collective-permute-start(bf16[7,34,1,128]{3,0,2,1:T(8,128)(2,1)S(1)} %get-tuple-element.68), channel_id=1, source_target_pairs={{0,1},{1,0},{2,3},{3,2},{4,5},{5,4},{6,7},{7,6},{8,9},{9,8},{10,11... | collective-permute-start | bytes 182792 | tf_op jit(solution)/shard_map/ppermute | solution.py:41
  62.3 2.3 %collective-permute-done.8 = bf16[7,34,1,128]{3,0,2,1:T(8,128)(2,1)S(1)} collective-permute-done((bf16[7,34,1,128]{3,0,2,1:T(8,128)(2,1)S(1)}, bf16[7,34,1,128]{3,0,2,1:T(8,128)(2,1)S(1)}, u32[]{:S(2)}, u32[]{:S(2)}) %collective-permute-start.8) | collective-permute-done | bytes 60960 | tf_op jit(solution)/shard_map/ppermute | solution.py:41
  64.6 1.3 %collective-permute-done.9 = bf16[7,34,1,128]{3,0,2,1:T(8,128)(2,1)S(1)} collective-permute-done((bf16[7,34,1,128]{3,0,2,1:T(8,128)(2,1)S(1)}, bf16[7,34,1,128]{3,0,2,1:T(8,128)(2,1)S(1)}, u32[]{:S(2)}, u32[]{:S(2)}) %collective-permute-start.9) | collective-permute-done | bytes 60960 | tf_op jit(solution)/shard_map/ppermute | solution.py:44
  65.8 1.3 %maximum_convert_fusion.1 = f32[7,34,34,128]{3,0,2,1:T(8,128)S(1)} fusion(bf16[7,34,1,128]{3,0,2,1:T(8,128)(2,1)S(1)} %collective-permute-done.9, bf16[7,1,32,128]{3,0,2,1:T(8,128)(2,1)S(1)} %collective-permute-done.7, bf16[7,32,32,128]{3,0,2,1:T(8,128)(2,1)S(1)} %get-tuple-element.54, bf16[7,1,32,128]{3,0,2,1:T(8,128)(2,1)S(1)} %collective-permute-done.6, ...), kind=kLoop, calls=%fused_computation.33 | loop fusion | flops 5178880 | bytes 6214656 | tf_op jit(solution)/shard_map/convert_element_type | solution.py:113
  67.2 1.2 %fusion.19 = f32[1,34,34,128]{3,0,2,1:T(1,128)S(1)} fusion(f32[7,34,34,128]{3,0,2,1:T(8,128)S(1)} %fusion.34), kind=kLoop, calls=%fused_computation.36 | loop fusion | flops 147968 | bytes 1183744 | tf_op jit(solution)/shard_map/exp | solution.py:50
  70.8 3.5 %fusion.50 = (f32[7,32,32,1]{3,0,2,1:T(8,128)S(1)}, f32[7,32,32,1]{3,0,2,1:T(8,128)}) fusion(f32[7,34,34,128]{3,0,2,1:T(8,128)S(1)} %fusion.34), kind=kLoop, calls=%fused_computation.109 | loop fusion | bytes 114688 | tf_op jit(solution)/shard_map/jit(_roll_static)/slice | solution.py:61
  74.3 4.8 %fusion.49 = (f32[7,32,32,127]{3,0,2,1:T(8,128)}, f32[7,32,32,127]{3,0,2,1:T(8,128)}) fusion(f32[7,34,34,128]{3,0,2,1:T(8,128)S(1)} %fusion.34), kind=kLoop, calls=%fused_computation.108 | loop fusion | bytes 14565376 | tf_op jit(solution)/shard_map/jit(_roll_static)/slice | solution.py:61
  79.2 5.0 %fusion.25 = (f32[1,32,32,128]{3,0,2,1:T(1,128)S(1)}, f32[1,32,32,128]{3,0,2,1:T(1,128)S(1)}, f32[1,32,32,128]{3,0,2,1:T(1,128)S(1)}, f32[1,32,32,128]{3,0,2,1:T...) fusion(f32[1,34,34,128]{3,0,2,1:T(1,128)S(1)} %fusion.19, f32[1,32,32,127]{3,0,2,1:T(1,128)S(1)} %get-tuple-element.84, ...), kind=kLoop, calls=%fused_computation.47 | loop fusion | flops 1835008 | bytes 6815744 | tf_op jit(solution)/shard_map/mul | solution.py:65
  84.2 12.1 %fusion.17 = f32[1,7,32,32,128]{4,1,3,2,0:T(8,128)S(1)} fusion(f32[1,7,32,32,128]{4,3,2,1,0:T(8,128)S(1)} %copy-done, f32[7,32,32,128]{3,0,2,1:T(8,128)S(1)} %get-tuple-element.55, f32[7,32,32,127]{3,0,2,1:T(8,128)} %get-tuple-element.61, f32[7,32,32,1]{3,0,2,1:T(8,128)} %get-tuple-element.63, f32[7,32,32,1]{3,0,2,1:T(8,128)S(1)} %get-tuple-element.62, ...), kind=kLoop, calls=%fused_computation.31 | loop fusion | flops 25690112 | bytes 39977044 | tf_op jit(solution)/shard_map/broadcast_in_dim | solution.py:119
  96.2 2.5 %copy.15 = f32[1,7,32,32,128]{4,3,2,1,0:T(8,128)} copy(f32[1,7,32,32,128]{4,1,3,2,0:T(8,128)S(1)} %fusion.17) | data formatting | bytes 7340032 | tf_op jit(solution)/shard_map/broadcast_in_dim | solution.py:119
  (57 shorter events, 11.1 us)
Async XLA Ops:
  0.0 11.3 %copy-start.6 = (u32[32]{0:T(128)S(1)}, u32[32]{0:T(128)}, u32[]{:S(2)}) copy-start(u32[32]{0:T(128)} %constant.162) | copy-start | bytes 388
  0.0 12.5 %copy-start.5 = (s32[32]{0:T(128)S(1)}, s32[32]{0:T(128)}, u32[]{:S(2)}) copy-start(s32[32]{0:T(128)} %param.19) | copy-start | bytes 388
  0.0 18.0 %copy-start.3 = (f32[2,7]{1,0:T(2,128)S(1)}, f32[2,7]{1,0:T(2,128)}, u32[]{:S(2)}) copy-start(f32[2,7]{1,0:T(2,128)} %param.16) | copy-start | bytes 172
  0.0 18.0 %copy-start.2 = (s32[32,32,128]{2,1,0:T(8,128)S(1)}, s32[32,32,128]{2,1,0:T(8,128)}, u32[]{:S(2)}) copy-start(s32[32,32,128]{2,1,0:T(8,128)} %param.18) | copy-start | bytes 1572868
  0.0 18.1 %copy-start.4 = (f32[2,7]{1,0:T(2,128)S(1)}, f32[2,7]{1,0:T(2,128)}, u32[]{:S(2)}) copy-start(f32[2,7]{1,0:T(2,128)} %param.17) | copy-start | bytes 172
  5.4 12.7 %collective-permute-start.4 = (bf16[7,32,128]{2,0,1:T(8,128)(2,1)S(1)}, bf16[7,32,128]{2,0,1:T(8,128)(2,1)S(1)}, u32[]{:S(2)}, u32[]{:S(2)}) collective-permute-start(bf16[7,32,128]{2,0,1:T(8,128)(2,1)S(1)} %get-tuple-element.74), channel_id=1, source_target_pairs={{0,16},{16,0},{1,17},{17,1},{2,18},{18,2},{3,19},{19,3},{4,20},{20... | collective-permute-start | bytes 172040 | tf_op jit(solution)/shard_map/ppermute | solution.py:32
  8.5 11.3 %collective-permute-start.1 = (bf16[7,1,32,128]{3,0,2,1:T(8,128)(2,1)S(1)}, bf16[7,1,32,128]{3,0,2,1:T(8,128)(2,1)S(1)}, u32[]{:S(2)}, u32[]{:S(2)}) collective-permute-start(bf16[7,1,32,128]{3,0,2,1:T(8,128)(2,1)S(1)} %get-tuple-element.75), channel_id=1, source_target_pairs={{2,0},{4,2},{6,4},{8,6},{10,8},{12,10},{14,12},{0,14},{3,1},{5,3},... | collective-permute-start | bytes 172040 | tf_op jit(solution)/shard_map/ppermute | solution.py:44
  11.2 8.5 %collective-permute-start = (bf16[7,1,32,128]{3,0,2,1:T(8,128)(2,1)S(1)}, bf16[7,1,32,128]{3,0,2,1:T(8,128)(2,1)S(1)}, u32[]{:S(2)}, u32[]{:S(2)}) collective-permute-start(bf16[7,1,32,128]{3,0,2,1:T(8,128)(2,1)S(1)} %get-tuple-element.76), channel_id=1, source_target_pairs={{0,2},{2,4},{4,6},{6,8},{8,10},{10,12},{12,14},{14,0},{1,3},{3,5},... | collective-permute-start | bytes 172040 | tf_op jit(solution)/shard_map/ppermute | solution.py:41
  18.1 24.5 %copy-start.1 = (pred[32,32,128]{2,1,0:T(8,128)(4,1)}, pred[32,32,128]{2,1,0:T(8,128)(4,1)S(1)}, u32[]{:S(2)}) copy-start(pred[32,32,128]{2,1,0:T(8,128)(4,1)S(1)} %compare_and_fusion) | copy-start | bytes 393220
  18.2 4.3 %collective-permute-start.5 = (bf16[7,32,128]{2,0,1:T(8,128)(2,1)S(1)}, bf16[7,32,128]{2,0,1:T(8,128)(2,1)S(1)}, u32[]{:S(2)}, u32[]{:S(2)}) collective-permute-start(bf16[7,32,128]{2,0,1:T(8,128)(2,1)S(1)} %collective-permute-done.4), channel_id=1, source_target_pairs={{0,1},{1,0},{2,3},{3,2},{4,5},{5,4},{6,7},{7,6},{8,9},{9,8},{10,11... | collective-permute-start | bytes 172040 | tf_op jit(solution)/shard_map/ppermute | solution.py:15
  19.8 4.4 %collective-permute-start.2 = (bf16[7,34,1,128]{3,0,2,1:T(8,128)(2,1)S(1)}, bf16[7,34,1,128]{3,0,2,1:T(8,128)(2,1)S(1)}, u32[]{:S(2)}, u32[]{:S(2)}) collective-permute-start(bf16[7,34,1,128]{3,0,2,1:T(8,128)(2,1)S(1)} %get-tuple-element.70), channel_id=1, source_target_pairs={{0,1},{1,0},{2,3},{3,2},{4,5},{5,4},{6,7},{7,6},{8,9},{9,8},{10,11... | collective-permute-start | bytes 182792 | tf_op jit(solution)/shard_map/ppermute | solution.py:41
  20.4 4.5 %collective-permute-start.3 = (bf16[7,34,1,128]{3,0,2,1:T(8,128)(2,1)S(1)}, bf16[7,34,1,128]{3,0,2,1:T(8,128)(2,1)S(1)}, u32[]{:S(2)}, u32[]{:S(2)}) collective-permute-start(bf16[7,34,1,128]{3,0,2,1:T(8,128)(2,1)S(1)} %get-tuple-element.71), channel_id=1, source_target_pairs={{1,0},{0,1},{3,2},{2,3},{5,4},{4,5},{7,6},{6,7},{9,8},{8,9},{11,10... | collective-permute-start | bytes 182792 | tf_op jit(solution)/shard_map/ppermute | solution.py:44
  38.2 4.4 %copy-start = (f32[1,7,32,32,128]{4,3,2,1,0:T(8,128)S(1)}, f32[1,7,32,32,128]{4,3,2,1,0:T(8,128)}, u32[]{:S(2)}) copy-start(f32[1,7,32,32,128]{4,3,2,1,0:T(8,128)} %param.15) | copy-start | bytes 11010052
  54.5 5.6 %collective-permute-start.6 = (bf16[7,1,32,128]{3,0,2,1:T(8,128)(2,1)S(1)}, bf16[7,1,32,128]{3,0,2,1:T(8,128)(2,1)S(1)}, u32[]{:S(2)}, u32[]{:S(2)}) collective-permute-start(bf16[7,1,32,128]{3,0,2,1:T(8,128)(2,1)S(1)} %get-tuple-element.72), channel_id=1, source_target_pairs={{0,2},{2,4},{4,6},{6,8},{8,10},{10,12},{12,14},{14,0},{1,3},{3,5},... | collective-permute-start | bytes 172040 | tf_op jit(solution)/shard_map/ppermute | solution.py:41
  54.6 5.6 %collective-permute-start.7 = (bf16[7,1,32,128]{3,0,2,1:T(8,128)(2,1)S(1)}, bf16[7,1,32,128]{3,0,2,1:T(8,128)(2,1)S(1)}, u32[]{:S(2)}, u32[]{:S(2)}) collective-permute-start(bf16[7,1,32,128]{3,0,2,1:T(8,128)(2,1)S(1)} %get-tuple-element.73), channel_id=1, source_target_pairs={{2,0},{4,2},{6,4},{8,6},{10,8},{12,10},{14,12},{0,14},{3,1},{5,3},... | collective-permute-start | bytes 172040 | tf_op jit(solution)/shard_map/ppermute | solution.py:44
  60.2 4.4 %collective-permute-start.8 = (bf16[7,34,1,128]{3,0,2,1:T(8,128)(2,1)S(1)}, bf16[7,34,1,128]{3,0,2,1:T(8,128)(2,1)S(1)}, u32[]{:S(2)}, u32[]{:S(2)}) collective-permute-start(bf16[7,34,1,128]{3,0,2,1:T(8,128)(2,1)S(1)} %get-tuple-element.68), channel_id=1, source_target_pairs={{0,1},{1,0},{2,3},{3,2},{4,5},{5,4},{6,7},{7,6},{8,9},{9,8},{10,11... | collective-permute-start | bytes 182792 | tf_op jit(solution)/shard_map/ppermute | solution.py:41
  61.5 4.3 %collective-permute-start.9 = (bf16[7,34,1,128]{3,0,2,1:T(8,128)(2,1)S(1)}, bf16[7,34,1,128]{3,0,2,1:T(8,128)(2,1)S(1)}, u32[]{:S(2)}, u32[]{:S(2)}) collective-permute-start(bf16[7,34,1,128]{3,0,2,1:T(8,128)(2,1)S(1)} %get-tuple-element.69), channel_id=1, source_target_pairs={{1,0},{0,1},{3,2},{2,3},{5,4},{4,5},{7,6},{6,7},{9,8},{8,9},{11,10... | collective-permute-start | bytes 182792 | tf_op jit(solution)/shard_map/ppermute | solution.py:44
